TPU v7x, 128 devices: a whole 4x4x4 slice. The times are simulated.
128 devices in a mesh: seq: 32 (over y_lo, z, x), head: 4 (over y_hi, core).
Axes of the slice: x: 4, y: 4 (y_hi: 2, y_lo: 2; y = y_hi * 2 + y_lo), z: 4, core: 2. Of those that a mesh axis runs over, the one named last changes fastest.
Arguments:
- tokens: bfloat16 [4096, 7168], P('seq', 'head'), may hold values from -6 to 6
- latent_down: bfloat16 [7168, 576], P('head'), may hold values from -0.0625 to 0.0625
- latent_gain: float32 [512], replicated, may hold values from 0.5 to 1.5
- query_nope: bfloat16 [4096, 8192], P('seq', 'head'), may hold values from -200 to 200
- query_rope: bfloat16 [4096, 4096], P('seq', 'head'), may hold values from -6 to 6
- key_up: bfloat16 [64, 128, 512], P('head'), may hold values from -0.5 to 0.5
- value_up: bfloat16 [64, 512, 128], P('head'), may hold values from -0.25 to 0.25
- prefix_latent: bfloat16 [2048, 576], P('seq'), may hold values from -6 to 6
- prefix_length: int32 [1], replicated, may hold values from 1024 to 2048
- page_table: int32 [256], replicated, may hold values from 0 to 255, each once
Outputs:
- attended: bfloat16 [4096, 8192], P('seq', 'head')
- decode_pool: bfloat16 [256, 9216], P('seq')
Inputs may be any that keep to these rules, and one draw needn't show every extreme that they name: The prefix rows from prefix_length[0] on are not live. `page_table`: A permutation of the 256 decode slots.
All inputs are finite; a program needn't handle non-finite values.
Results may differ from a plain program's by a relative error of at most 0.015.
Values may be sent and summed in bfloat16 or wider, within the bound.
A program may use at most 128 MiB of HBM per device.

v0:
```python
import jax
import jax.numpy as jnp
from jax import lax
from jax.sharding import PartitionSpec as P

LATENT = 512
ROPE = 64
NOPE = 128
VHEAD = 128
PAGE = 16


def sent_to_all(value, axis):
    copies = jnp.broadcast_to(value, (lax.axis_size(axis), *value.shape))
    return lax.all_to_all(copies, axis, split_axis=0, concat_axis=0, tiled=True)


def of_everyone(value, axis):
    return sent_to_all(value, axis).astype(jnp.float32).sum(axis=0)


def in_order(parts, dim):
    lengths = list(parts.shape[1:])
    lengths[dim] *= parts.shape[0]
    return jnp.moveaxis(parts, 0, dim).reshape(lengths)


def gather_directly(value, axis, dim):
    parts = sent_to_all(value, axis)
    return in_order(parts, dim)


def angles(positions):
    half_width = ROPE // 2
    frequency = 10000.0 ** (-jnp.arange(half_width, dtype=jnp.float32) / half_width)
    return positions.astype(jnp.float32)[:, None] * frequency[None, :]


def rotate(values, angle_table):
    half_width = values.shape[-1] // 2
    first = values[..., :half_width]
    second = values[..., half_width:]
    cosine = jnp.cos(angle_table)
    sinus = jnp.sin(angle_table)
    return jnp.concatenate(
        [first * cosine - second * sinus, first * sinus + second * cosine], axis=-1
    )


def finish(mixed, latent_gain, positions):
    latent = mixed[:, :LATENT]
    rope_part = mixed[:, LATENT:]
    normed = (
        latent * lax.rsqrt(jnp.mean(latent * latent, axis=1, keepdims=True) + 1e-06) * latent_gain
    )
    return jnp.concatenate(
        [normed.astype(jnp.bfloat16), rotate(rope_part, angles(positions)).astype(jnp.bfloat16)],
        axis=1,
    )


def per_device(
    tokens,
    latent_down,
    latent_gain,
    query_nope,
    query_rope,
    key_up,
    value_up,
    prefix_latent,
    prefix_length,
    page_table,
):
    row_count = tokens.shape[0]
    head_count = key_up.shape[0]
    row_width = LATENT + ROPE
    queries_dev = row_count * head_count
    seq_index = lax.axis_index("seq")
    offset = prefix_length[0]
    first_row = seq_index * row_count
    positions = offset + first_row + jnp.arange(row_count, dtype=jnp.int32)
    partial_terms = jnp.dot(tokens, latent_down, preferred_element_type=jnp.float32)
    mixed = of_everyone(partial_terms.astype(jnp.bfloat16), "head").astype(jnp.float32)
    new_keys = finish(mixed, latent_gain, positions)
    lifted = jnp.einsum(
        "thn,hnl->thl",
        query_nope.reshape(row_count, head_count, NOPE),
        key_up,
        preferred_element_type=jnp.float32,
    ).astype(jnp.bfloat16)
    turned = rotate(
        query_rope.reshape(row_count, head_count, ROPE).astype(jnp.float32),
        angles(positions)[:, None, :],
    ).astype(jnp.bfloat16)
    queries = jnp.concatenate([lifted, turned], axis=2).reshape(queries_dev, row_width)
    query_token = first_row + jnp.arange(queries_dev, dtype=jnp.int32) // head_count
    score_scale = (NOPE + ROPE) ** (-0.5)

    def attend(state, key_rows, live_mask):
        running_top, denominator, running = state
        scores = (
            lax.dot_general(
                key_rows, queries, (((1,), (1,)), ((), ())), preferred_element_type=jnp.float32
            )
            * score_scale
        )
        new_top = jnp.maximum(running_top, jnp.max(jnp.where(live_mask, scores, -1e30), axis=0))
        weights = jnp.where(live_mask, jnp.exp(scores - new_top[None, :]), 0.0)
        fading = jnp.exp(running_top - new_top)
        denominator = denominator * fading + jnp.sum(weights, axis=0)
        update = lax.dot_general(
            weights.astype(jnp.bfloat16),
            key_rows[:, :LATENT],
            (((0,), (0,)), ((), ())),
            preferred_element_type=jnp.float32,
        )
        return (new_top, denominator, running * fading[:, None] + update)

    def guarded(state, key_rows, live_mask):
        return attend(state, key_rows, live_mask)

    def sweep_keys(state, key_rows, live_rule):
        total_rows = key_rows.shape[0]
        blocks = key_rows.reshape(total_rows // 512, 512, row_width)
        starts = 512 * jnp.arange(total_rows // 512, dtype=jnp.int32)

        def advance(inner_state, block_pair):
            key_block, block_start = block_pair
            key_index = block_start + jnp.arange(512, dtype=jnp.int32)
            return (guarded(inner_state, key_block, live_rule(key_index)), None)

        state, unused = lax.scan(advance, state, (blocks, starts))
        return state

    def prefix_rule(key_index):
        return jnp.broadcast_to((key_index < offset)[:, None], (key_index.shape[0], queries_dev))

    def group_rule(key_index):
        return key_index[:, None] <= query_token[None, :]

    prefix_all = gather_directly(prefix_latent, "seq", 0)
    state = (
        jnp.full((queries_dev,), -1e30, jnp.float32),
        jnp.zeros((queries_dev,), jnp.float32),
        jnp.zeros((queries_dev, LATENT), jnp.float32),
    )
    state = sweep_keys(state, prefix_all, prefix_rule)
    pages_dev = row_count // PAGE
    page_width = PAGE * row_width
    all_keys = lax.all_gather(new_keys, "seq", axis=0, tiled=True)
    state = sweep_keys(state, all_keys, group_rule)
    axis_size = lax.axis_size("seq")
    targets = lax.dynamic_slice_in_dim(page_table, seq_index * pages_dev, pages_dev)
    slot_ids = jnp.arange(axis_size * pages_dev, dtype=jnp.int32)
    select = (slot_ids[:, None] == targets[None, :]).astype(jnp.bfloat16)
    outgoing = jnp.dot(
        select, new_keys.reshape(pages_dev, page_width), preferred_element_type=jnp.float32
    ).astype(jnp.bfloat16)
    incoming = lax.all_to_all(outgoing, "seq", split_axis=0, concat_axis=0, tiled=True)
    decode_pool = jnp.sum(
        incoming.reshape(axis_size, pages_dev, page_width), axis=0, dtype=jnp.float32
    )
    running_top, denominator, running = state
    attention = (
        (running / denominator[:, None]).astype(jnp.bfloat16).reshape(row_count, head_count, LATENT)
    )
    output = jnp.einsum("thl,hlv->thv", attention, value_up, preferred_element_type=jnp.float32)
    attended = output.astype(jnp.bfloat16).reshape(row_count, head_count * VHEAD)
    return (attended, decode_pool.astype(jnp.bfloat16))


def solution(mesh):
    placed = (
        P("seq", "head"),
        P("head", None),
        P(),
        P("seq", "head"),
        P("seq", "head"),
        P("head", None, None),
        P("head", None, None),
        P("seq", None),
        P(),
        P(),
    )
    return jax.shard_map(
        per_device,
        mesh=mesh,
        in_specs=placed,
        out_specs=(P("seq", "head"), P("seq", None)),
        check_vma=False,
    )
```

profile of v0, /device:TPU:32, one launch (start us, length us, event | category | flops | bytes accessed | tf_op | source)
XLA Modules:
  0.0 342.1 jit_solution(6677885738440692457)
XLA Ops:
  16.0 10.1 %all-to-all-done.1 = bf16[4,128,576]{1,2,0:T(8,128)(2,1)S(1)} async-done(((bf16[4,128,576]{1,2,0:T(8,128)(2,1)}), bf16[4,128,576]{1,2,0:T(8,128)(2,1)S(1)}, u32[]{:S(2)}, u32[]{:S(2)}) %all-to-all-start.1) | async-done | bytes 589856 | tf_op jit(solution)/shard_map/all_to_all | solution.py:15
  28.9 8.2 %all-to-all-start = ((bf16[32,64,576]{2,1,0:T(8,128)(2,1)}), bf16[32,64,576]{2,1,0:T(8,128)(2,1)}, u32[]{:S(2)}, u32[]{:S(2)}) async-start(bf16[32,64,576]{2,1,0:T(8,128)(2,1)} %broadcast_in_dim.53), calls=%async_computation | async-start | bytes 5242880 | tf_op jit(solution)/shard_map/all_to_all | solution.py:15
  45.9 4.9 %copy.42 = bf16[128,16,576]{2,1,0:T(8,128)(2,1)} copy(bf16[128,16,576]{0,2,1:T(8,128)(2,1)} %pad_maximum_fusion) | data formatting | bytes 4718592 | tf_op jit(solution)/shard_map/concatenate | solution.py:95
  54.4 20.2 %all-to-all-done = bf16[32,64,576]{2,1,0:T(8,128)(2,1)} async-done(((bf16[32,64,576]{2,1,0:T(8,128)(2,1)}), bf16[32,64,576]{2,1,0:T(8,128)(2,1)}, u32[]{:S(2)}, u32[]{:S(2)}) %all-to-all-start) | async-done | bytes 2359328 | tf_op jit(solution)/shard_map/all_to_all | solution.py:15
  74.6 7.5 %all-to-all-start.2 = ((bf16[32,8,9216]{2,1,0:T(8,128)(2,1)}), bf16[32,8,9216]{2,1,0:T(8,128)(2,1)}, u32[]{:S(2)}, u32[]{:S(2)}) async-start(bf16[32,8,9216]{2,1,0:T(8,128)(2,1)} %fusion.30), calls=%async_computation.2 | async-start | bytes 9437184 | tf_op jit(solution)/shard_map/all_to_all | solution.py:159
  82.1 65.6 %while.31 = (s32[]{:T(128)}, f32[2048]{0:T(1024)S(1)}, f32[2048]{0:T(1024)S(1)}, f32[2048,512]{1,0:T(8,128)}, s32[4]{0:T(128)S(1)}, /*index=5*/s32[]{:T(128)}, b...) while((s32[]{:T(128)}, f32[2048]{0:T(1024)S(1)}, ...), condition=%wide.region_3.4_spmd.clone, body=%wide.region_0.3_spmd.clone.sunk | while | flops 2296392704 | bytes 42535076 | solution.py:132
  85.1 5.7 %select_reduce_fusion.2 = (f32[2048]{0:T(1024)S(1)}, f32[512,2048]{1,0:T(8,128)}) fusion(pred[512]{0:T(512)(128)(4,1)S(1)} %add_compare_fusion.2, bf16[512,576]{1,0:T(8,128)(2,1)S(1)} %dynamic-slice_bitcast_fusion.5, bf16[2048,576]{1,0:T(8,128)(2,1)} %get-tuple-element.343), kind=kOutput, calls=%fused_computation.30.clone.1 | convolution fusion | flops 1211103232 | bytes 7152128 | tf_op jit(solution)/shard_map/while/body/eval_jaxpr/dot_general | solution.py:102
  100.3 5.7 %select_reduce_fusion.2 = (f32[2048]{0:T(1024)S(1)}, f32[512,2048]{1,0:T(8,128)}) fusion(pred[512]{0:T(512)(128)(4,1)S(1)} %add_compare_fusion.2, bf16[512,576]{1,0:T(8,128)(2,1)S(1)} %dynamic-slice_bitcast_fusion.5, bf16[2048,576]{1,0:T(8,128)(2,1)} %get-tuple-element.343), kind=kOutput, calls=%fused_computation.30.clone.1 | convolution fusion | flops 1211103232 | bytes 7152128 | tf_op jit(solution)/shard_map/while/body/eval_jaxpr/dot_general | solution.py:102
  109.5 4.7 %fusion.76 = f32[2048,512]{1,0:T(8,128)} fusion(f32[2048,512]{1,0:T(8,128)} %get-tuple-element.329, f32[512,2048]{1,0:T(8,128)S(1)} %copy-done.1, f32[2048]{0:T(1024)S(1)} %get-tuple-element.315, f32[2048]{0:T(1024)S(1)} %select_maximum_fusion.2, pred[512]{0:T(512)(128)(4,1)S(1)} %add_compare_fusion.2, pred[]{:T(512)S(6)} %compare.5, ...), kind=kOutput, calls=%fused_computation.28.clone.1 | convolution fusion | flops 1081081856 | bytes 13124097 | tf_op jit(solution)/shard_map/while/body/eval_jaxpr/dot_general | solution.py:111
  117.1 5.7 %select_reduce_fusion.2 = (f32[2048]{0:T(1024)S(1)}, f32[512,2048]{1,0:T(8,128)}) fusion(pred[512]{0:T(512)(128)(4,1)S(1)} %add_compare_fusion.2, bf16[512,576]{1,0:T(8,128)(2,1)S(1)} %dynamic-slice_bitcast_fusion.5, bf16[2048,576]{1,0:T(8,128)(2,1)} %get-tuple-element.343), kind=kOutput, calls=%fused_computation.30.clone.1 | convolution fusion | flops 1211103232 | bytes 7152128 | tf_op jit(solution)/shard_map/while/body/eval_jaxpr/dot_general | solution.py:102
  126.2 4.7 %fusion.76 = f32[2048,512]{1,0:T(8,128)} fusion(f32[2048,512]{1,0:T(8,128)} %get-tuple-element.329, f32[512,2048]{1,0:T(8,128)S(1)} %copy-done.1, f32[2048]{0:T(1024)S(1)} %get-tuple-element.315, f32[2048]{0:T(1024)S(1)} %select_maximum_fusion.2, pred[512]{0:T(512)(128)(4,1)S(1)} %add_compare_fusion.2, pred[]{:T(512)S(6)} %compare.5, ...), kind=kOutput, calls=%fused_computation.28.clone.1 | convolution fusion | flops 1081081856 | bytes 13124097 | tf_op jit(solution)/shard_map/while/body/eval_jaxpr/dot_general | solution.py:111
  133.8 5.7 %select_reduce_fusion.2 = (f32[2048]{0:T(1024)S(1)}, f32[512,2048]{1,0:T(8,128)}) fusion(pred[512]{0:T(512)(128)(4,1)S(1)} %add_compare_fusion.2, bf16[512,576]{1,0:T(8,128)(2,1)S(1)} %dynamic-slice_bitcast_fusion.5, bf16[2048,576]{1,0:T(8,128)(2,1)} %get-tuple-element.343), kind=kOutput, calls=%fused_computation.30.clone.1 | convolution fusion | flops 1211103232 | bytes 7152128 | tf_op jit(solution)/shard_map/while/body/eval_jaxpr/dot_general | solution.py:102
  143.1 4.7 %fusion.76 = f32[2048,512]{1,0:T(8,128)} fusion(f32[2048,512]{1,0:T(8,128)} %get-tuple-element.329, f32[512,2048]{1,0:T(8,128)S(1)} %copy-done.1, f32[2048]{0:T(1024)S(1)} %get-tuple-element.315, f32[2048]{0:T(1024)S(1)} %select_maximum_fusion.2, pred[512]{0:T(512)(128)(4,1)S(1)} %add_compare_fusion.2, pred[]{:T(512)S(6)} %compare.5, ...), kind=kOutput, calls=%fused_computation.28.clone.1 | convolution fusion | flops 1081081856 | bytes 13124097 | tf_op jit(solution)/shard_map/while/body/eval_jaxpr/dot_general | solution.py:111
  147.7 6.9 %all-to-all-done.2 = bf16[32,8,9216]{2,1,0:T(8,128)(2,1)} async-done(((bf16[32,8,9216]{2,1,0:T(8,128)(2,1)}), bf16[32,8,9216]{2,1,0:T(8,128)(2,1)}, u32[]{:S(2)}, u32[]{:S(2)}) %all-to-all-start.2) | async-done | bytes 4718624 | tf_op jit(solution)/shard_map/all_to_all | solution.py:159
  158.4 69.1 %all-gather.2.cloned.1.call-done = bf16[4096,576]{0,1:T(8,128)(2,1)} async-done(((bf16[128,576]{0,1:T(8,128)(2,1)}), bf16[4096,576]{0,1:T(8,128)(2,1)}) %all-gather.2.cloned.1.call-update) | async-done | bytes 4718608 | tf_op jit(solution)/shard_map/all_gather | solution.py:150
  227.5 7.6 %copy.50 = bf16[4096,576]{1,0:T(8,128)(2,1)} copy(bf16[4096,576]{0,1:T(8,128)(2,1)} %all-gather.2.cloned.1.call-done) | data formatting | bytes 9437184
  235.1 93.6 %while.30 = (s32[]{:T(128)}, f32[2048]{0:T(1024)S(1)}, f32[2048]{0:T(1024)S(1)}, f32[2048,512]{1,0:T(8,128)}, s32[8]{0:T(128)S(1)}, /*index=5*/bf16[8,512,576]{2...) while((s32[]{:T(128)}, f32[2048]{0:T(1024)S(1)}, f32[2048]{0:T(1024)S(1)}, ...), condition=%wide.region_9.10_spmd.clone, body=%wide.region_6.9_spmd.clone.sunk | while | flops 2298501632 | bytes 25796724 | solution.py:132
  242.2 4.6 %multiply_add_fusion.5 = f32[2048,512]{1,0:T(8,128)} fusion(f32[2048,512]{1,0:T(8,128)} %get-tuple-element.358, f32[512,2048]{1,0:T(8,128)S(1)} %get-tuple-element.301, f32[2048]{0:T(1024)S(1)} %get-tuple-element.303, f32[2048]{0:T(1024)S(1)} %max.11, s32[2048]{0:T(1024)S(1)} %fusion.67, s32[512]{0:T(512)S(1)} %iota_add_fusion.2, ...), kind=kOutput, calls=%fused_computation.4.clone.1 | convolution fusion | flops 1081081856 | bytes 13133824 | tf_op jit(solution)/shard_map/while/body/eval_jaxpr/dot_general | solution.py:111
  265.6 4.6 %multiply_add_fusion.5 = f32[2048,512]{1,0:T(8,128)} fusion(f32[2048,512]{1,0:T(8,128)} %get-tuple-element.358, f32[512,2048]{1,0:T(8,128)S(1)} %get-tuple-element.301, f32[2048]{0:T(1024)S(1)} %get-tuple-element.303, f32[2048]{0:T(1024)S(1)} %max.11, s32[2048]{0:T(1024)S(1)} %fusion.67, s32[512]{0:T(512)S(1)} %iota_add_fusion.2, ...), kind=kOutput, calls=%fused_computation.4.clone.1 | convolution fusion | flops 1081081856 | bytes 13133824 | tf_op jit(solution)/shard_map/while/body/eval_jaxpr/dot_general | solution.py:111
  277.3 4.6 %multiply_add_fusion.5 = f32[2048,512]{1,0:T(8,128)} fusion(f32[2048,512]{1,0:T(8,128)} %get-tuple-element.358, f32[512,2048]{1,0:T(8,128)S(1)} %get-tuple-element.301, f32[2048]{0:T(1024)S(1)} %get-tuple-element.303, f32[2048]{0:T(1024)S(1)} %max.11, s32[2048]{0:T(1024)S(1)} %fusion.67, s32[512]{0:T(512)S(1)} %iota_add_fusion.2, ...), kind=kOutput, calls=%fused_computation.4.clone.1 | convolution fusion | flops 1081081856 | bytes 13133824 | tf_op jit(solution)/shard_map/while/body/eval_jaxpr/dot_general | solution.py:111
  289.0 4.6 %multiply_add_fusion.5 = f32[2048,512]{1,0:T(8,128)} fusion(f32[2048,512]{1,0:T(8,128)} %get-tuple-element.358, f32[512,2048]{1,0:T(8,128)S(1)} %get-tuple-element.301, f32[2048]{0:T(1024)S(1)} %get-tuple-element.303, f32[2048]{0:T(1024)S(1)} %max.11, s32[2048]{0:T(1024)S(1)} %fusion.67, s32[512]{0:T(512)S(1)} %iota_add_fusion.2, ...), kind=kOutput, calls=%fused_computation.4.clone.1 | convolution fusion | flops 1081081856 | bytes 13133824 | tf_op jit(solution)/shard_map/while/body/eval_jaxpr/dot_general | solution.py:111
  300.7 4.6 %multiply_add_fusion.5 = f32[2048,512]{1,0:T(8,128)} fusion(f32[2048,512]{1,0:T(8,128)} %get-tuple-element.358, f32[512,2048]{1,0:T(8,128)S(1)} %get-tuple-element.301, f32[2048]{0:T(1024)S(1)} %get-tuple-element.303, f32[2048]{0:T(1024)S(1)} %max.11, s32[2048]{0:T(1024)S(1)} %fusion.67, s32[512]{0:T(512)S(1)} %iota_add_fusion.2, ...), kind=kOutput, calls=%fused_computation.4.clone.1 | convolution fusion | flops 1081081856 | bytes 13133824 | tf_op jit(solution)/shard_map/while/body/eval_jaxpr/dot_general | solution.py:111
  312.4 4.6 %multiply_add_fusion.5 = f32[2048,512]{1,0:T(8,128)} fusion(f32[2048,512]{1,0:T(8,128)} %get-tuple-element.358, f32[512,2048]{1,0:T(8,128)S(1)} %get-tuple-element.301, f32[2048]{0:T(1024)S(1)} %get-tuple-element.303, f32[2048]{0:T(1024)S(1)} %max.11, s32[2048]{0:T(1024)S(1)} %fusion.67, s32[512]{0:T(512)S(1)} %iota_add_fusion.2, ...), kind=kOutput, calls=%fused_computation.4.clone.1 | convolution fusion | flops 1081081856 | bytes 13133824 | tf_op jit(solution)/shard_map/while/body/eval_jaxpr/dot_general | solution.py:111
  324.1 4.6 %multiply_add_fusion.5 = f32[2048,512]{1,0:T(8,128)} fusion(f32[2048,512]{1,0:T(8,128)} %get-tuple-element.358, f32[512,2048]{1,0:T(8,128)S(1)} %get-tuple-element.301, f32[2048]{0:T(1024)S(1)} %get-tuple-element.303, f32[2048]{0:T(1024)S(1)} %max.11, s32[2048]{0:T(1024)S(1)} %fusion.67, s32[512]{0:T(512)S(1)} %iota_add_fusion.2, ...), kind=kOutput, calls=%fused_computation.4.clone.1 | convolution fusion | flops 1081081856 | bytes 13133824 | tf_op jit(solution)/shard_map/while/body/eval_jaxpr/dot_general | solution.py:111
  (151 shorter events, 123.1 us)
Async XLA Ops:
  7.2 30.0 %copy-start = (bf16[16,128,512]{2,1,0:T(8,128)(2,1)S(1)}, bf16[16,128,512]{2,1,0:T(8,128)(2,1)}, u32[]{:S(2)}) copy-start(bf16[16,128,512]{2,1,0:T(8,128)(2,1)} %param.19) | copy-start | bytes 6291460
  7.2 8.6 %copy-start.2 = (bf16[128,1024]{1,0:T(8,128)(2,1)S(1)}, bf16[128,1024]{1,0:T(8,128)(2,1)}, u32[]{:S(2)}) copy-start(bf16[128,1024]{1,0:T(8,128)(2,1)} %param.18) | copy-start | bytes 786436
  7.2 8.8 %copy-start.5 = (s32[256]{0:T(256)S(1)}, s32[256]{0:T(256)}, u32[]{:S(2)}) copy-start(s32[256]{0:T(256)} %param.23) | copy-start | bytes 3076
  10.7 15.5 %all-to-all-start.1 = ((bf16[4,128,576]{1,2,0:T(8,128)(2,1)}), bf16[4,128,576]{1,2,0:T(8,128)(2,1)S(1)}, u32[]{:S(2)}, u32[]{:S(2)}) async-start(bf16[4,128,576]{1,2,0:T(8,128)(2,1)} %broadcast_in_dim.54), calls=%async_computation.1 | async-start | bytes 1179648 | tf_op jit(solution)/shard_map/all_to_all | solution.py:15
  28.9 45.7 %all-to-all-start = ((bf16[32,64,576]{2,1,0:T(8,128)(2,1)}), bf16[32,64,576]{2,1,0:T(8,128)(2,1)}, u32[]{:S(2)}, u32[]{:S(2)}) async-start(bf16[32,64,576]{2,1,0:T(8,128)(2,1)} %broadcast_in_dim.53), calls=%async_computation | async-start | bytes 5242880 | tf_op jit(solution)/shard_map/all_to_all | solution.py:15
  37.1 3.6 %copy-start.3 = (f32[512]{0:T(512)S(1)}, f32[512]{0:T(512)}, u32[]{:S(2)}) copy-start(f32[512]{0:T(512)} %param.16) | copy-start | bytes 6148
  37.1 190.4 %all-gather.2.cloned.1.call-start = ((), (), s32[]{:S(2)}) async-start(), calls=%async_computation.3 | async-start | bytes 4866048 | tf_op jit(solution)/shard_map/all_gather | solution.py:150
  74.6 80.1 %all-to-all-start.2 = ((bf16[32,8,9216]{2,1,0:T(8,128)(2,1)}), bf16[32,8,9216]{2,1,0:T(8,128)(2,1)}, u32[]{:S(2)}, u32[]{:S(2)}) async-start(bf16[32,8,9216]{2,1,0:T(8,128)(2,1)} %fusion.30), calls=%async_computation.2 | async-start | bytes 9437184 | tf_op jit(solution)/shard_map/all_to_all | solution.py:159
  90.8 3.4 %copy-start.1 = (f32[512,2048]{1,0:T(8,128)S(1)}, f32[512,2048]{1,0:T(8,128)}, u32[]{:S(2)}) copy-start(f32[512,2048]{1,0:T(8,128)} %get-tuple-element.313) | copy-start | bytes 12582916 | tf_op jit(solution)/shard_map/while
  106.0 3.5 %copy-start.1 = (f32[512,2048]{1,0:T(8,128)S(1)}, f32[512,2048]{1,0:T(8,128)}, u32[]{:S(2)}) copy-start(f32[512,2048]{1,0:T(8,128)} %get-tuple-element.313) | copy-start | bytes 12582916 | tf_op jit(solution)/shard_map/while
  122.8 3.4 %copy-start.1 = (f32[512,2048]{1,0:T(8,128)S(1)}, f32[512,2048]{1,0:T(8,128)}, u32[]{:S(2)}) copy-start(f32[512,2048]{1,0:T(8,128)} %get-tuple-element.313) | copy-start | bytes 12582916 | tf_op jit(solution)/shard_map/while
  139.6 3.5 %copy-start.1 = (f32[512,2048]{1,0:T(8,128)S(1)}, f32[512,2048]{1,0:T(8,128)}, u32[]{:S(2)}) copy-start(f32[512,2048]{1,0:T(8,128)} %get-tuple-element.313) | copy-start | bytes 12582916 | tf_op jit(solution)/shard_map/while
  328.7 2.9 copy-start.4
Sparse Core Ops, SparseCore 0:
  41.6 185.7 all-gather.1
where the time goes:
time: 344 us; the launch traced here: 342 us
  matrix products  118 us (34%)
  waiting for transfers between devices  106 us (31%)
  other arithmetic  41.8 us (12%)
  local copies, waits for them, and re-layouts  40.5 us (12%)
  starting transfers between devices  20.2 us (6%)
  between operations  14.9 us (4%)
    all_gather x1, waiting for transfers between devices, per_device(): all_keys = lax.all_gather(new_keys, 'seq', axis=0, tiled=True)  69.1 us
    dot_general x12, matrix products, attend(): lax.dot_general(weights.astype(jnp.bfloat16), key_rows[:, :LATENT], (((0,...  53.9 us
    dot_general x12, matrix products, attend(): lax.dot_general(key_rows, queries, (((1,), (1,)), ((), ())), preferred_el...  52 us
    all_to_all x2, waiting for transfers between devices, sent_to_all(): return lax.all_to_all(copies, axis, split_axis=0, concat_axis=0, tiled=True)  30.3 us
    reduce_sum x12, other arithmetic, attend(): denominator = denominator * fading + jnp.sum(weights, axis=0)  20.7 us
    squeeze x12, local copies, waits for them, and re-layouts, sweep_keys(): state, unused = lax.scan(advance, state, (blocks, starts))  13.8 us
    all_to_all x2, starting transfers between devices, sent_to_all(): return lax.all_to_all(copies, axis, split_axis=0, concat_axis=0, tiled=True)  12.7 us
    unnamed x12, local copies, waits for them, and re-layouts  8.82 us
  transfers between devices with their start and end apart: 4, of which 4 were waited for; matrix products, arithmetic and copies ran while one was open for 25% of the time, Pallas kernels for 0%

commit v1 on v0

--- a/solution.py
+++ b/solution.py
@@ -147,7 +147,8 @@
     state = sweep_keys(state, prefix_all, prefix_rule)
     pages_dev = row_count // PAGE
     page_width = PAGE * row_width
-    all_keys = lax.all_gather(new_keys, "seq", axis=0, tiled=True)
+    sent = jnp.stack([new_keys] * lax.axis_size("seq"))
+    all_keys = jnp.concatenate(lax.all_to_all(sent, "seq", 0, 0), axis=0)
     state = sweep_keys(state, all_keys, group_rule)
     axis_size = lax.axis_size("seq")
     targets = lax.dynamic_slice_in_dim(page_table, seq_index * pages_dev, pages_dev)

time: 344 us -> 264 us (0.77)
  waiting for transfers between devices: 106 us -> 33.1 us
  local copies, waits for them, and re-layouts: 40.5 us -> 80.3 us
  matrix products: 118 us -> 84.7 us
  between operations: 14.9 us -> 1.47 us
  other arithmetic: 41.8 us -> 32 us
  starting transfers between devices: 20.2 us -> 29 us
    all_gather x1 -> x0, waiting for transfers between devices: 69.1 us -> none  [per_device(): all_keys = lax.all_gather(new_keys, 'seq', axis=0, tiled=True)]
    while x20 -> x60, local copies, waits for them, and re-layouts: 0.95 us -> 38.4 us
    dot_general x12, matrix products: 53.9 us -> 28.9 us  [attend(): lax.dot_general(weights.astype(jnp.bfloat16), key_rows[:, :LATENT], (((0,...]
    reduce_sum x12, other arithmetic: 20.7 us -> 11.3 us  [attend(): denominator = denominator * fading + jnp.sum(weights, axis=0)]
    dot_general x12, matrix products: 52 us -> 43.9 us  [attend(): lax.dot_general(key_rows, queries, (((1,), (1,)), ((), ())), preferred_el...]
    all_to_all x1, waiting for transfers between devices: 6.93 us -> 0.01 us  [per_device(): lax.all_to_all(outgoing, 'seq', split_axis=0, concat_axis=0, tiled=True)]
    all_to_all x0 -> x1, starting transfers between devices: none -> 6.71 us  [per_device(): all_keys = jnp.concatenate(lax.all_to_all(sent, 'seq', 0, 0), axis=0)]
    all_to_all x0 -> x1, waiting for transfers between devices: none -> 6.24 us  [per_device(): all_keys = jnp.concatenate(lax.all_to_all(sent, 'seq', 0, 0), axis=0)]
  transfers between devices with their start and end apart: 4 -> 4, of which waited for: 4 -> 3; matrix products, arithmetic and copies ran while one was open for 25% -> 56% of each run, Pallas kernels for 0% -> 0%
where the time goes in v1:
time: 264 us; the launch traced here: 262 us
  matrix products  84.7 us (32%)
  local copies, waits for them, and re-layouts  80.3 us (30%)
  waiting for transfers between devices  33.1 us (13%)
  other arithmetic  32 us (12%)
  starting transfers between devices  29 us (11%)
    dot_general x12, matrix products, attend(): lax.dot_general(key_rows, queries, (((1,), (1,)), ((), ())), preferred_el...  43.9 us
    while x60, local copies, waits for them, and re-layouts  38.4 us
    dot_general x12, matrix products, attend(): lax.dot_general(weights.astype(jnp.bfloat16), key_rows[:, :LATENT], (((0,...  28.9 us
    all_to_all x2, waiting for transfers between devices, sent_to_all(): return lax.all_to_all(copies, axis, split_axis=0, concat_axis=0, tiled=True)  26.9 us
    squeeze x12, local copies, waits for them, and re-layouts, sweep_keys(): state, unused = lax.scan(advance, state, (blocks, starts))  13.8 us
    all_to_all x2, starting transfers between devices, sent_to_all(): return lax.all_to_all(copies, axis, split_axis=0, concat_axis=0, tiled=True)  12.7 us
    reduce_sum x12, other arithmetic, attend(): denominator = denominator * fading + jnp.sum(weights, axis=0)  11.3 us
    all_to_all x1, starting transfers between devices, per_device(): lax.all_to_all(outgoing, 'seq', split_axis=0, concat_axis=0, tiled=True)  9.65 us
  transfers between devices with their start and end apart: 4, of which 3 were waited for; matrix products, arithmetic and copies ran while one was open for 56% of the time, Pallas kernels for 0%

profile of v1, /device:TPU:32, one launch (start us, length us, event | category | flops | bytes accessed | tf_op | source)
XLA Modules:
  0.0 261.5 jit_solution(4975550243524191540)
XLA Ops:
  4.1 4.5 %all-to-all-start.1 = ((bf16[4,128,576]{1,2,0:T(8,128)(2,1)}), bf16[4,128,576]{1,2,0:T(8,128)(2,1)S(1)}, u32[]{:S(2)}, u32[]{:S(2)}) async-start(bf16[4,128,576]{1,2,0:T(8,128)(2,1)} %broadcast_in_dim.54), calls=%async_computation.1 | async-start | bytes 1179648 | tf_op jit(solution)/shard_map/all_to_all | solution.py:15
  9.5 10.1 %all-to-all-done.1 = bf16[4,128,576]{1,2,0:T(8,128)(2,1)S(1)} async-done(((bf16[4,128,576]{1,2,0:T(8,128)(2,1)}), bf16[4,128,576]{1,2,0:T(8,128)(2,1)S(1)}, u32[]{:S(2)}, u32[]{:S(2)}) %all-to-all-start.1) | async-done | bytes 589856 | tf_op jit(solution)/shard_map/all_to_all | solution.py:15
  22.3 8.2 %all-to-all-start = ((bf16[32,64,576]{2,1,0:T(8,128)(2,1)}), bf16[32,64,576]{2,1,0:T(8,128)(2,1)}, u32[]{:S(2)}, u32[]{:S(2)}) async-start(bf16[32,64,576]{2,1,0:T(8,128)(2,1)} %broadcast_in_dim.53), calls=%async_computation | async-start | bytes 5242880 | tf_op jit(solution)/shard_map/all_to_all | solution.py:15
  37.9 4.9 %copy.55 = bf16[128,16,576]{2,1,0:T(8,128)(2,1)} copy(bf16[128,16,576]{0,2,1:T(8,128)(2,1)} %pad_maximum_fusion) | data formatting | bytes 4718592 | tf_op jit(solution)/shard_map/concatenate | solution.py:95
  46.3 16.8 %all-to-all-done = bf16[32,64,576]{2,1,0:T(8,128)(2,1)} async-done(((bf16[32,64,576]{2,1,0:T(8,128)(2,1)}), bf16[32,64,576]{2,1,0:T(8,128)(2,1)}, u32[]{:S(2)}, u32[]{:S(2)}) %all-to-all-start) | async-done | bytes 2359328 | tf_op jit(solution)/shard_map/all_to_all | solution.py:15
  66.3 6.7 %all-to-all-start.2 = ((bf16[32,128,576]{1,2,0:T(8,128)(2,1)}), bf16[32,128,576]{1,2,0:T(8,128)(2,1)}, u32[]{:S(2)}, u32[]{:S(2)}) async-start(bf16[32,128,576]{1,2,0:T(8,128)(2,1)} %stack.2), calls=%async_computation.2 | async-start | bytes 9437184 | tf_op jit(solution)/shard_map/all_to_all | solution.py:151
  73.0 52.7 %while.31 = (s32[]{:T(128)}, f32[2048]{0:T(1024)S(1)}, f32[2048]{0:T(1024)S(1)}, f32[2048,512]{1,0:T(8,128)}, s32[4]{0:T(128)S(1)}, /*index=5*/s32[]{:T(128)}, b...) while((s32[]{:T(128)}, f32[2048]{0:T(1024)S(1)}, ...), condition=%wide.region_3.4_spmd.clone, body=%wide.region_0.3_spmd.clone.sunk | while | flops 2296392704 | bytes 59312328 | solution.py:132
  76.0 3.7 %select_reduce_fusion.2 = (f32[2048]{0:T(1024)S(1)}, f32[512,2048]{1,0:T(8,128)S(1)}) fusion(pred[512]{0:T(512)(128)(4,1)S(1)} %add_compare_fusion.2, bf16[512,576]{1,0:T(8,128)(2,1)S(1)} %dynamic-slice_bitcast_fusion.5, bf16[2048,576]{1,0:T(8,128)(2,1)} %get-tuple-element.353), kind=kOutput, calls=%fused_computation.30.clone.1 | convolution fusion | flops 1211103232 | bytes 7152128 | tf_op jit(solution)/shard_map/while/body/eval_jaxpr/dot_general | solution.py:102
  89.2 3.7 %select_reduce_fusion.2 = (f32[2048]{0:T(1024)S(1)}, f32[512,2048]{1,0:T(8,128)S(1)}) fusion(pred[512]{0:T(512)(128)(4,1)S(1)} %add_compare_fusion.2, bf16[512,576]{1,0:T(8,128)(2,1)S(1)} %dynamic-slice_bitcast_fusion.5, bf16[2048,576]{1,0:T(8,128)(2,1)} %get-tuple-element.353), kind=kOutput, calls=%fused_computation.30.clone.1 | convolution fusion | flops 1211103232 | bytes 7152128 | tf_op jit(solution)/shard_map/while/body/eval_jaxpr/dot_general | solution.py:102
  102.4 3.7 %select_reduce_fusion.2 = (f32[2048]{0:T(1024)S(1)}, f32[512,2048]{1,0:T(8,128)S(1)}) fusion(pred[512]{0:T(512)(128)(4,1)S(1)} %add_compare_fusion.2, bf16[512,576]{1,0:T(8,128)(2,1)S(1)} %dynamic-slice_bitcast_fusion.5, bf16[2048,576]{1,0:T(8,128)(2,1)} %get-tuple-element.353), kind=kOutput, calls=%fused_computation.30.clone.1 | convolution fusion | flops 1211103232 | bytes 7152128 | tf_op jit(solution)/shard_map/while/body/eval_jaxpr/dot_general | solution.py:102
  115.6 3.7 %select_reduce_fusion.2 = (f32[2048]{0:T(1024)S(1)}, f32[512,2048]{1,0:T(8,128)S(1)}) fusion(pred[512]{0:T(512)(128)(4,1)S(1)} %add_compare_fusion.2, bf16[512,576]{1,0:T(8,128)(2,1)S(1)} %dynamic-slice_bitcast_fusion.5, bf16[2048,576]{1,0:T(8,128)(2,1)} %get-tuple-element.353), kind=kOutput, calls=%fused_computation.30.clone.1 | convolution fusion | flops 1211103232 | bytes 7152128 | tf_op jit(solution)/shard_map/while/body/eval_jaxpr/dot_general | solution.py:102
  125.7 6.2 %all-to-all-done.2 = bf16[32,128,576]{1,2,0:T(8,128)(2,1)} async-done(((bf16[32,128,576]{1,2,0:T(8,128)(2,1)}), bf16[32,128,576]{1,2,0:T(8,128)(2,1)}, u32[]{:S(2)}, u32[]{:S(2)}) %all-to-all-start.2) | async-done | bytes 4718624 | tf_op jit(solution)/shard_map/all_to_all | solution.py:151
  132.0 9.6 %all-to-all-start.3 = ((bf16[32,8,9216]{2,1,0:T(8,128)(2,1)}), bf16[32,8,9216]{2,1,0:T(8,128)(2,1)}, u32[]{:S(2)}, u32[]{:S(2)}) async-start(bf16[32,8,9216]{2,1,0:T(8,128)(2,1)} %fusion.30), calls=%async_computation.3 | async-start | bytes 9437184 | tf_op jit(solution)/shard_map/all_to_all | solution.py:160
  141.6 7.7 %copy.64 = bf16[32,128,576]{2,1,0:T(8,128)(2,1)} copy(bf16[32,128,576]{1,2,0:T(8,128)(2,1)} %all-to-all-done.2) | data formatting | bytes 9437184
  149.3 102.0 %while.30 = (s32[]{:T(128)}, f32[2048]{0:T(1024)S(1)}, f32[2048]{0:T(1024)S(1)}, f32[2048,512]{1,0:T(8,128)}, s32[8]{0:T(128)S(1)}, /*index=5*/bf16[8,512,576]{2...) while((s32[]{:T(128)}, f32[2048]{0:T(1024)S(1)}, f32[2048]{0:T(1024)S(1)}, ...), condition=%wide.region_9.10_spmd.clone, body=%wide.region_6.9_spmd.clone.sunk | while | flops 2298501632 | bytes 59351220 | solution.py:132
  151.7 3.7 %fusion.68 = (f32[2048]{0:T(1024)S(1)}, f32[512,2048]{1,0:T(8,128)S(1)}) fusion(s32[2048]{0:T(1024)S(1)} %fusion.67, s32[512]{0:T(512)S(1)} %iota_add_fusion.2, bf16[512,576]{1,0:T(8,128)(2,1)S(1)} %dynamic-slice_bitcast_fusion.4, bf16[2048,576]{1,0:T(8,128)(2,1)} %get-tuple-element.380), kind=kOutput, calls=%fused_computation.3.clone.1 | convolution fusion | flops 1212151808 | bytes 7161856 | tf_op jit(solution)/shard_map/while/body/eval_jaxpr/dot_general | solution.py:102
  164.4 3.7 %fusion.68 = (f32[2048]{0:T(1024)S(1)}, f32[512,2048]{1,0:T(8,128)S(1)}) fusion(s32[2048]{0:T(1024)S(1)} %fusion.67, s32[512]{0:T(512)S(1)} %iota_add_fusion.2, bf16[512,576]{1,0:T(8,128)(2,1)S(1)} %dynamic-slice_bitcast_fusion.4, bf16[2048,576]{1,0:T(8,128)(2,1)} %get-tuple-element.380), kind=kOutput, calls=%fused_computation.3.clone.1 | convolution fusion | flops 1212151808 | bytes 7161856 | tf_op jit(solution)/shard_map/while/body/eval_jaxpr/dot_general | solution.py:102
  177.2 3.6 %fusion.68 = (f32[2048]{0:T(1024)S(1)}, f32[512,2048]{1,0:T(8,128)S(1)}) fusion(s32[2048]{0:T(1024)S(1)} %fusion.67, s32[512]{0:T(512)S(1)} %iota_add_fusion.2, bf16[512,576]{1,0:T(8,128)(2,1)S(1)} %dynamic-slice_bitcast_fusion.4, bf16[2048,576]{1,0:T(8,128)(2,1)} %get-tuple-element.380), kind=kOutput, calls=%fused_computation.3.clone.1 | convolution fusion | flops 1212151808 | bytes 7161856 | tf_op jit(solution)/shard_map/while/body/eval_jaxpr/dot_general | solution.py:102
  189.9 3.7 %fusion.68 = (f32[2048]{0:T(1024)S(1)}, f32[512,2048]{1,0:T(8,128)S(1)}) fusion(s32[2048]{0:T(1024)S(1)} %fusion.67, s32[512]{0:T(512)S(1)} %iota_add_fusion.2, bf16[512,576]{1,0:T(8,128)(2,1)S(1)} %dynamic-slice_bitcast_fusion.4, bf16[2048,576]{1,0:T(8,128)(2,1)} %get-tuple-element.380), kind=kOutput, calls=%fused_computation.3.clone.1 | convolution fusion | flops 1212151808 | bytes 7161856 | tf_op jit(solution)/shard_map/while/body/eval_jaxpr/dot_general | solution.py:102
  202.7 3.6 %fusion.68 = (f32[2048]{0:T(1024)S(1)}, f32[512,2048]{1,0:T(8,128)S(1)}) fusion(s32[2048]{0:T(1024)S(1)} %fusion.67, s32[512]{0:T(512)S(1)} %iota_add_fusion.2, bf16[512,576]{1,0:T(8,128)(2,1)S(1)} %dynamic-slice_bitcast_fusion.4, bf16[2048,576]{1,0:T(8,128)(2,1)} %get-tuple-element.380), kind=kOutput, calls=%fused_computation.3.clone.1 | convolution fusion | flops 1212151808 | bytes 7161856 | tf_op jit(solution)/shard_map/while/body/eval_jaxpr/dot_general | solution.py:102
  215.4 3.7 %fusion.68 = (f32[2048]{0:T(1024)S(1)}, f32[512,2048]{1,0:T(8,128)S(1)}) fusion(s32[2048]{0:T(1024)S(1)} %fusion.67, s32[512]{0:T(512)S(1)} %iota_add_fusion.2, bf16[512,576]{1,0:T(8,128)(2,1)S(1)} %dynamic-slice_bitcast_fusion.4, bf16[2048,576]{1,0:T(8,128)(2,1)} %get-tuple-element.380), kind=kOutput, calls=%fused_computation.3.clone.1 | convolution fusion | flops 1212151808 | bytes 7161856 | tf_op jit(solution)/shard_map/while/body/eval_jaxpr/dot_general | solution.py:102
  228.2 3.6 %fusion.68 = (f32[2048]{0:T(1024)S(1)}, f32[512,2048]{1,0:T(8,128)S(1)}) fusion(s32[2048]{0:T(1024)S(1)} %fusion.67, s32[512]{0:T(512)S(1)} %iota_add_fusion.2, bf16[512,576]{1,0:T(8,128)(2,1)S(1)} %dynamic-slice_bitcast_fusion.4, bf16[2048,576]{1,0:T(8,128)(2,1)} %get-tuple-element.380), kind=kOutput, calls=%fused_computation.3.clone.1 | convolution fusion | flops 1212151808 | bytes 7161856 | tf_op jit(solution)/shard_map/while/body/eval_jaxpr/dot_general | solution.py:102
  240.9 3.7 %fusion.68 = (f32[2048]{0:T(1024)S(1)}, f32[512,2048]{1,0:T(8,128)S(1)}) fusion(s32[2048]{0:T(1024)S(1)} %fusion.67, s32[512]{0:T(512)S(1)} %iota_add_fusion.2, bf16[512,576]{1,0:T(8,128)(2,1)S(1)} %dynamic-slice_bitcast_fusion.4, bf16[2048,576]{1,0:T(8,128)(2,1)} %get-tuple-element.380), kind=kOutput, calls=%fused_computation.3.clone.1 | convolution fusion | flops 1212151808 | bytes 7161856 | tf_op jit(solution)/shard_map/while/body/eval_jaxpr/dot_general | solution.py:102
  257.8 3.7 %reduce_sum.50 = bf16[8,9216]{1,0:T(8,128)(2,1)} reduce(bf16[32,8,9216]{2,1,0:T(8,128)(2,1)} %all-to-all-done.3, bf16[]{:T(256)} %constant.81.clone.1), dimensions={0}, to_apply=%region_10.11 | reduce | flops 2285568 | bytes 4866050 | tf_op jit(solution)/shard_map/reduce_sum | solution.py:161
  (191 shorter events, 136.9 us)
Async XLA Ops:
  0.6 30.0 %copy-start = (bf16[16,128,512]{2,1,0:T(8,128)(2,1)S(1)}, bf16[16,128,512]{2,1,0:T(8,128)(2,1)}, u32[]{:S(2)}) copy-start(bf16[16,128,512]{2,1,0:T(8,128)(2,1)} %param.19) | copy-start | bytes 6291460
  0.6 8.6 %copy-start.5 = (bf16[128,1024]{1,0:T(8,128)(2,1)S(1)}, bf16[128,1024]{1,0:T(8,128)(2,1)}, u32[]{:S(2)}) copy-start(bf16[128,1024]{1,0:T(8,128)(2,1)} %param.18) | copy-start | bytes 786436
  0.7 8.8 %copy-start.8 = (s32[256]{0:T(256)S(1)}, s32[256]{0:T(256)}, u32[]{:S(2)}) copy-start(s32[256]{0:T(256)} %param.23) | copy-start | bytes 3076
  4.1 15.5 %all-to-all-start.1 = ((bf16[4,128,576]{1,2,0:T(8,128)(2,1)}), bf16[4,128,576]{1,2,0:T(8,128)(2,1)S(1)}, u32[]{:S(2)}, u32[]{:S(2)}) async-start(bf16[4,128,576]{1,2,0:T(8,128)(2,1)} %broadcast_in_dim.54), calls=%async_computation.1 | async-start | bytes 1179648 | tf_op jit(solution)/shard_map/all_to_all | solution.py:15
  22.3 40.8 %all-to-all-start = ((bf16[32,64,576]{2,1,0:T(8,128)(2,1)}), bf16[32,64,576]{2,1,0:T(8,128)(2,1)}, u32[]{:S(2)}, u32[]{:S(2)}) async-start(bf16[32,64,576]{2,1,0:T(8,128)(2,1)} %broadcast_in_dim.53), calls=%async_computation | async-start | bytes 5242880 | tf_op jit(solution)/shard_map/all_to_all | solution.py:15
  30.5 3.5 %copy-start.6 = (f32[512]{0:T(512)S(1)}, f32[512]{0:T(512)}, u32[]{:S(2)}) copy-start(f32[512]{0:T(512)} %param.16) | copy-start | bytes 6148
  66.3 65.7 %all-to-all-start.2 = ((bf16[32,128,576]{1,2,0:T(8,128)(2,1)}), bf16[32,128,576]{1,2,0:T(8,128)(2,1)}, u32[]{:S(2)}, u32[]{:S(2)}) async-start(bf16[32,128,576]{1,2,0:T(8,128)(2,1)} %stack.2), calls=%async_computation.2 | async-start | bytes 9437184 | tf_op jit(solution)/shard_map/all_to_all | solution.py:151
  79.7 2.2 copy-start.1
  84.2 2.0 copy-start.2
  92.9 2.2 copy-start.1
  97.4 2.0 copy-start.2
  106.1 2.2 copy-start.1
  110.5 2.0 copy-start.2
  119.2 2.2 copy-start.1
  132.0 125.9 %all-to-all-start.3 = ((bf16[32,8,9216]{2,1,0:T(8,128)(2,1)}), bf16[32,8,9216]{2,1,0:T(8,128)(2,1)}, u32[]{:S(2)}, u32[]{:S(2)}) async-start(bf16[32,8,9216]{2,1,0:T(8,128)(2,1)} %fusion.30), calls=%async_computation.3 | async-start | bytes 9437184 | tf_op jit(solution)/shard_map/all_to_all | solution.py:160
  155.3 2.2 copy-start.3
  168.1 2.2 copy-start.3
  180.8 2.2 copy-start.3
  193.6 2.2 copy-start.3
  206.3 2.2 copy-start.3
  219.1 2.2 copy-start.3
  231.8 2.2 copy-start.3
  244.6 2.2 copy-start.3
  251.3 2.9 %copy-start.7 = (bf16[16,512,128]{2,1,0:T(8,128)(2,1)S(1)}, bf16[16,512,128]{2,1,0:T(8,128)(2,1)}, u32[]{:S(2)}) copy-start(bf16[16,512,128]{2,1,0:T(8,128)(2,1)} %param.20) | copy-start | bytes 6291460
  (9 other events, 18.1 us)
